TPU v7x, 256 devices: a whole 4x4x8 slice. The times are simulated.
256 devices in a mesh: region: 32 (over x, z), comm: 8 (over y, core).
Axes of the slice: x: 4, y: 4, z: 8, core: 2. Of those that a mesh axis runs over, the one named last changes fastest.
Arguments:
- cost: float32 [128, 262144], P('comm', 'region'), may hold values from 0.01 to 15, as said below
- flow_start: float32 [128, 262144], P('comm', 'region'), may hold values from 0 to 0.5
- capacity: float32 [262144], P('region'), may hold values from 5 to 135, as said below
- cap_dual_start: float32 [262144], P('region'), may hold values from 0 to 1
- demand: float32 [128, 131072], P('comm', 'region'), may hold values from -24 to 24
- node_dual_start: float32 [128, 131072], P('comm', 'region'), may hold values from -6 to 6
- incidence: float32 [4096, 128, 128], P('region'), may hold values from -0.25 to 0.25
- block_node: int32 [4096], P('region'), may hold values from 0 to 39
- ghost_source: int32 [256], P('region'), may hold values from 0 to 127, as said below
Outputs:
- final_flow: float32 [128, 262144], P('comm', 'region')
- final_cap_dual: float32 [262144], P('region')
- final_node_dual: float32 [128, 131072], P('comm', 'region')
Inputs may be any that keep to these rules, and one draw needn't show every extreme that they name: Each cost is positive. Each capacity is positive. `ghost_source`: ghost slot g of region r names boundary block j of region q as q * 4 + j. Slot 0 of every region has q = r + 16 in cyclic order; every other slot has q at most two regions from r in cyclic order (q may be r).
All inputs are finite; a program needn't handle non-finite values.
Results may differ from a plain program's by a relative error of at most 0.00021.
Values sent between devices are 32-bit elements; how exact they have to be, the bound alone decides.
A program may use at most 64 MiB of HBM per device.

v0:
```python
import jax
import jax.numpy as jnp
from jax import lax
from jax.sharding import PartitionSpec as P

BPA = 2
NBD = 4
NG = 8
ITERS = 2
step_scale = 0.08
highest = lax.Precision.HIGHEST


def pick_blocks(bnd_table, indices, commodities, count, block_width):
    return jnp.take(bnd_table.reshape(commodities, count, block_width), indices, axis=1)


def body(
    cost,
    flow_start,
    capacity,
    cap_dual_start,
    demand,
    node_dual_start,
    incidence,
    block_node,
    ghost_source,
):
    commodities, arc_count = cost.shape
    block_count, block_width, _ = incidence.shape
    own_blocks = demand.shape[1] // block_width
    region_total = lax.axis_size("region")
    bound_all = region_total * NBD
    slot_count = own_blocks + NG
    cost_sq = jnp.sum(cost * cost)
    demand_sq = jnp.sum(demand * demand)
    capacity_sq = jnp.sum(capacity * capacity)
    cost_all, demand_all = lax.psum((cost_sq, demand_sq), ("region", "comm"))
    capacity_all = lax.psum(capacity_sq, "region")
    weight = jnp.sqrt(cost_all / (demand_all + capacity_all))
    primal_step = step_scale / weight
    dual_step = step_scale * weight
    slot_table = (block_node[:, None] == jnp.arange(slot_count, dtype=jnp.int32)[None, :]).astype(
        jnp.float32
    )
    ghost_table = (ghost_source[:, None] == jnp.arange(bound_all, dtype=jnp.int32)[None, :]).astype(
        jnp.float32
    )
    flow_now, cap_dual, node_dual = (flow_start, cap_dual_start, node_dual_start)
    edge_cols = NBD * block_width
    for iteration in range(ITERS):
        bnd_table = lax.all_gather(node_dual[:, :edge_cols], "region", axis=1, tiled=True)
        ghost_duals = pick_blocks(bnd_table, ghost_source, commodities, bound_all, block_width)
        dual_blocks = jnp.concatenate(
            [node_dual.reshape(commodities, own_blocks, block_width), ghost_duals], axis=1
        )
        chosen_duals = jnp.take(dual_blocks, block_node, axis=1)
        back_term = jnp.einsum("kbn,bna->kba", chosen_duals, incidence, precision=highest)
        back_term = (
            back_term.reshape(commodities, block_count // BPA, BPA, block_width)
            .sum(axis=2)
            .reshape(commodities, arc_count)
        )
        flow_new = jnp.maximum(flow_now - primal_step * (cost - back_term + cap_dual[None, :]), 0.0)
        flow_bar = 2.0 * flow_new - flow_now
        arc_load = jnp.sum(flow_bar, axis=0)
        load_total = lax.psum(arc_load, "comm")
        cap_dual = jnp.maximum(cap_dual + dual_step * (load_total - capacity), 0.0)
        repeated_flow = jnp.repeat(
            flow_bar.reshape(commodities, arc_count // block_width, block_width), BPA, axis=1
        )
        forward = jnp.einsum("kba,bna->kbn", repeated_flow, incidence, precision=highest)
        slot_rows = jnp.einsum("kbn,bs->ksn", forward, slot_table, precision=highest)
        own_rows = slot_rows[:, :own_blocks]
        routed = jnp.einsum(
            "kgn,gb->kbn", slot_rows[:, own_blocks:], ghost_table, precision=highest
        )
        arrived = lax.psum_scatter(routed, "region", scatter_dimension=1, tiled=True)
        node_rows = jnp.concatenate([own_rows[:, :NBD] + arrived, own_rows[:, NBD:]], axis=1)
        node_dual = node_dual + dual_step * (
            demand - node_rows.reshape(commodities, own_blocks * block_width)
        )
        flow_now = flow_new
    return (flow_now, cap_dual, node_dual)


def solution(mesh):
    return jax.shard_map(
        body,
        mesh=mesh,
        in_specs=(
            P("comm", "region"),
            P("comm", "region"),
            P("region"),
            P("region"),
            P("comm", "region"),
            P("comm", "region"),
            P("region", None, None),
            P("region"),
            P("region"),
        ),
        out_specs=(P("comm", "region"), P("region"), P("comm", "region")),
        check_vma=False,
    )
```

profile of v0, /device:TPU:8, one launch (start us, length us, event | category | flops | bytes accessed | tf_op | source)
XLA Modules:
  0.0 738.6 jit_solution(913210635620972559)
XLA Ops:
  7.2 1.5 slice.30
  8.7 0.0 reduce-scatter.3.cloned.1.call-start
  8.8 1.6 multiply_reduce_fusion.1
  10.4 1.8 multiply_reduce_fusion
  12.2 1.4 multiply_reduce_fusion.2
  13.6 79.2 %all-reduce = (f32[]{:T(128)}, f32[]{:T(128)}) all-reduce(f32[]{:T(128)} %multiply_reduce_fusion, f32[]{:T(128)} %multiply_reduce_fusion.1), channel_id=1, replica_groups=mesh['region'=32,'comm'=8] {'region','comm'}, use_global_device_ids=true, to_apply=%region_1.0 | all-reduce | flops 2 | bytes 16 | tf_op jit(solution)/shard_map/psum | solution.py:38
  92.9 73.2 %psum.37 = f32[]{:T(128)} all-reduce(f32[]{:T(128)} %multiply_reduce_fusion.2), channel_id=1, replica_groups=mesh['region'=32,'comm'=8] {'region'}, use_global_device_ids=true, to_apply=%region_5.0 | all-reduce | flops 1 | bytes 8 | tf_op jit(solution)/shard_map/psum | solution.py:39
  168.2 0.7 compare_select_fusion.1
  168.8 0.7 compare_select_fusion
  169.5 0.7 compare_and_fusion
  170.1 0.7 compare_and_fusion.1
  170.8 1.0 copy_bitcast_fusion.5
  171.8 1.3 copy_bitcast_fusion.1
  173.1 0.6 gather_fusion
  173.7 0.1 select_bitcast_fusion.1
  173.8 0.8 gather_fusion.1
  174.6 9.6 %bitcast_reduce_fusion.1 = f32[16,64,128]{2,0,1:T(8,128)S(1)} fusion(f32[128,128,128]{2,1,0:T(8,128)} %param.19, f32[128,16,128]{2,1,0:T(8,128)S(1)} %gather_fusion.1, pred[128]{0:T(512)(128)(4,1)S(1)} %compare_and_fusion), kind=kOutput, calls=%fused_computation.13 | convolution fusion | flops 403046400 | bytes 9961600 | tf_op jit(solution)/shard_map/kbn,bna->kba/dot_general | solution.py:58
  184.2 0.2 fusion.28
  184.5 0.1 copy_bitcast_fusion.3
  184.5 0.1 broadcast_in_dim.30
  184.7 15.4 %convolution_bitcast_fusion.1 = f32[16,128,128]{2,0,1:T(8,128)S(1)} fusion(f32[16,128,128]{2,0,1:T(8,128)S(1)} %bitcast.122, f32[128,128,128]{2,1,0:T(8,128)} %param.19), kind=kOutput, calls=%fused_computation.5 | convolution fusion | flops 402653184 | bytes 10485760 | tf_op jit(solution)/shard_map/kba,bna->kbn/dot_general | solution.py:72
  200.1 0.8 convolution_bitcast_fusion.5
  200.9 0.7 convolution_bitcast_fusion.3
  201.6 1.6 copy.37
  203.2 0.0 all-gather.5.cloned.1.call-start
  203.3 206.3 %reduce-scatter.3.cloned.1.call-done = f32[16,4,128]{2,0,1:T(8,128)} async-done(((f32[16,128,128]{2,0,1:T(8,128)}), f32[16,4,128]{2,0,1:T(8,128)}) %reduce-scatter.3.cloned.1.call-update) | async-done | bytes 32784 | tf_op jit(solution)/shard_map/reduce_scatter | solution.py:78
  409.6 0.8 slice_add_fusion.1
  410.4 0.2 fusion.27
  410.6 0.6 slice.49
  411.3 20.9 %psum.38 = f32[8192]{0:T(1024)S(1)} all-reduce(f32[8192]{0:T(1024)S(1)} %get-tuple-element.9), channel_id=1, replica_groups=mesh['region'=32,'comm'=8] {'comm'}, use_global_device_ids=true, to_apply=%region_10.13 | all-reduce | flops 8192 | bytes 65536 | tf_op jit(solution)/shard_map/psum | solution.py:67
  432.2 55.1 %all-gather.5.cloned.1.call-done = f32[16,16384]{1,0:T(8,128)} async-done(((f32[16,512]{1,0:T(8,128)}), f32[16,16384]{1,0:T(8,128)}) %all-gather.5.cloned.1.call-update) | async-done | bytes 1048592 | tf_op jit(solution)/shard_map/all_gather | solution.py:52
  487.3 1.3 copy_bitcast_fusion
  488.6 0.6 gather_fusion.2
  489.2 0.1 select_bitcast_fusion
  489.3 0.8 gather_fusion.3
  490.1 9.6 %bitcast_reduce_fusion = f32[16,64,128]{2,0,1:T(8,128)S(1)} fusion(f32[128,128,128]{2,1,0:T(8,128)} %param.19, f32[128,16,128]{2,1,0:T(8,128)S(1)} %gather_fusion.3, pred[128]{0:T(512)(128)(4,1)S(1)} %compare_and_fusion), kind=kOutput, calls=%fused_computation.12 | convolution fusion | flops 403046400 | bytes 9961600 | tf_op jit(solution)/shard_map/kbn,bna->kba/dot_general | solution.py:58
  499.7 0.2 fusion.30
  499.9 0.1 broadcast_in_dim.31
  500.0 15.4 %convolution_bitcast_fusion = f32[16,128,128]{2,0,1:T(8,128)S(1)} fusion(f32[16,128,128]{2,0,1:T(8,128)S(1)} %bitcast.123, f32[128,128,128]{2,1,0:T(8,128)} %param.19), kind=kOutput, calls=%fused_computation.4 | convolution fusion | flops 402653184 | bytes 10485760 | tf_op jit(solution)/shard_map/kba,bna->kbn/dot_general | solution.py:72
  515.4 0.8 convolution_bitcast_fusion.4
  516.2 0.7 convolution_bitcast_fusion.2
  516.9 1.6 copy.44
  518.5 0.1 fusion.31
  518.7 20.7 %psum.39 = f32[8192]{0:T(1024)S(1)} all-reduce(f32[8192]{0:T(1024)S(1)} %fusion.31), channel_id=1, replica_groups=mesh['region'=32,'comm'=8] {'comm'}, use_global_device_ids=true, to_apply=%region_12.15 | all-reduce | flops 8192 | bytes 65536 | tf_op jit(solution)/shard_map/psum | solution.py:67
  539.3 0.6 add_maximum_fusion
  540.0 190.4 %reduce-scatter.5.cloned.1.call-done = f32[16,4,128]{2,0,1:T(8,128)} async-done(((f32[16,128,128]{2,0,1:T(8,128)}), f32[16,4,128]{2,0,1:T(8,128)}) %reduce-scatter.5.cloned.1.call-update) | async-done | bytes 32784 | tf_op jit(solution)/shard_map/reduce_scatter | solution.py:78
  730.3 0.8 slice_add_fusion
  731.1 0.9 fusion.25
  (36 shorter events, 0.5 us)
Async XLA Ops:
  7.2 177.0 %copy-start = (f32[16,8192]{1,0:T(8,128)S(1)}, f32[16,8192]{1,0:T(8,128)}, u32[]{:S(2)}) copy-start(f32[16,8192]{1,0:T(8,128)} %param.13) | copy-start | bytes 1572868
  7.2 177.0 %copy-start.6 = (f32[8192]{0:T(1024)S(1)}, f32[8192]{0:T(1024)}, u32[]{:S(2)}) copy-start(f32[8192]{0:T(1024)} %param.16) | copy-start | bytes 98308
  7.2 177.0 %copy-start.2 = (f32[16,8192]{1,0:T(8,128)S(1)}, f32[16,8192]{1,0:T(8,128)}, u32[]{:S(2)}) copy-start(f32[16,8192]{1,0:T(8,128)} %param.14) | copy-start | bytes 1572868
  7.2 164.6 %all-gather.3.cloned.1.call-start = ((), (), s32[]{:S(2)}) async-start(), calls=%async_computation.2 | async-start | bytes 1081344 | tf_op jit(solution)/shard_map/all_gather | solution.py:52
  8.7 400.9 %reduce-scatter.3.cloned.1.call-start = ((), (), s32[]{:S(2)}) async-start(), calls=%async_computation.3 | async-start | bytes 1081344 | tf_op jit(solution)/shard_map/reduce_scatter | solution.py:78
  184.2 15.9 %copy-start.7 = (s32[128]{0:T(128)S(1)}, s32[128]{0:T(128)}, u32[]{:S(2)}) copy-start(s32[128]{0:T(128)} %param.20) | copy-start | bytes 1540
  184.2 16.6 %copy-start.8 = (s32[8]{0:T(128)S(1)}, s32[8]{0:T(128)}, u32[]{:S(2)}) copy-start(s32[8]{0:T(128)} %param.21) | copy-start | bytes 100
  184.6 225.8 %copy-start.1 = (f32[16,4096]{1,0:T(8,128)S(1)}, f32[16,4096]{1,0:T(8,128)}, u32[]{:S(2)}) copy-start(f32[16,4096]{1,0:T(8,128)} %param.17) | copy-start | bytes 786436
  184.6 225.8 %copy-start.4 = (f32[16,4096]{1,0:T(8,128)S(1)}, f32[16,4096]{1,0:T(8,128)}, u32[]{:S(2)}) copy-start(f32[16,4096]{1,0:T(8,128)} %param.18) | copy-start | bytes 786436
  184.6 247.5 %copy-start.5 = (f32[8192]{0:T(1024)S(1)}, f32[8192]{0:T(1024)}, u32[]{:S(2)}) copy-start(f32[8192]{0:T(1024)} %param.15) | copy-start | bytes 98308
  203.2 284.1 %all-gather.5.cloned.1.call-start = ((), (), s32[]{:S(2)}) async-start(), calls=%async_computation.4 | async-start | bytes 1081344 | tf_op jit(solution)/shard_map/all_gather | solution.py:52
  411.3 319.1 %reduce-scatter.5.cloned.1.call-start = ((), (), s32[]{:S(2)}) async-start(), calls=%async_computation.5 | async-start | bytes 1081344 | tf_op jit(solution)/shard_map/reduce_scatter | solution.py:78
  499.8 18.7 %copy-start.3 = (f32[16,8192]{1,0:T(8,128)}, f32[16,8192]{1,0:T(8,128)S(1)}, u32[]{:S(2)}) copy-start(f32[16,8192]{1,0:T(8,128)S(1)} %get-tuple-element.8) | copy-start | bytes 1572868
Sparse Core Ops, SparseCore 0:
  11.2 78.9 all-gather.2
  203.3 206.2 reduce-scatter.2
  412.8 74.4 all-gather.4
  518.6 211.6 reduce-scatter.4
where the time goes:
time: 739 us
  waiting for transfers between devices  452 us (61%)
  blocking collectives  194 us (26%)
  matrix products  53 us (7%)
  between operations  16.2 us (2%)
  local copies, waits for them, and re-layouts  11.8 us (2%)
  other arithmetic  11.5 us (2%)
    reduce_scatter x2, waiting for transfers between devices, body(): lax.psum_scatter(routed, 'region', scatter_dimension=1, tiled=True)  397 us
    psum x1, blocking collectives, body(): cost_all, demand_all = lax.psum((cost_sq, demand_sq), ('region', 'comm'))  79.2 us
    psum x1, blocking collectives, body(): capacity_all = lax.psum(capacity_sq, 'region')  73.2 us
    all_gather x2, waiting for transfers between devices, body(): lax.all_gather(node_dual[:, :edge_cols], 'region', axis=1, tiled=True)  55.1 us
    psum x2, blocking collectives, body(): load_total = lax.psum(arc_load, 'comm')  41.5 us
    dot_general x2, matrix products, body(): jnp.einsum('kba,bna->kbn', repeated_flow, incidence, precision=highest)  30.9 us
    dot_general x2, matrix products, body(): jnp.einsum('kbn,bna->kba', chosen_duals, incidence, precision=highest)  19.2 us
  transfers between devices with their start and end apart: 4, of which 3 were waited for; matrix products, arithmetic and copies ran while one was open for 1% of the time, Pallas kernels for 0%

commit v1 on v0

--- a/solution.py
+++ b/solution.py
@@ -64,7 +64,8 @@
         flow_new = jnp.maximum(flow_now - primal_step * (cost - back_term + cap_dual[None, :]), 0.0)
         flow_bar = 2.0 * flow_new - flow_now
         arc_load = jnp.sum(flow_bar, axis=0)
-        load_total = lax.psum(arc_load, "comm")
+        pieces = lax.all_gather(arc_load, "comm", axis=0, tiled=False)
+        load_total = pieces.sum(axis=0)
         cap_dual = jnp.maximum(cap_dual + dual_step * (load_total - capacity), 0.0)
         repeated_flow = jnp.repeat(
             flow_bar.reshape(commodities, arc_count // block_width, block_width), BPA, axis=1

time: 739 us -> 739 us (level)
  blocking collectives: 194 us -> 178 us
  waiting for transfers between devices: 452 us -> 467 us
    psum x2 -> x0, blocking collectives: 41.5 us -> none  [body(): load_total = lax.psum(arc_load, 'comm')]
    all_gather x0 -> x2, blocking collectives: none -> 25.9 us  [body(): pieces = lax.all_gather(arc_load, 'comm', axis=0, tiled=False)]
    all_gather x2, waiting for transfers between devices: 55.1 us -> 62.8 us  [body(): lax.all_gather(node_dual[:, :edge_cols], 'region', axis=1, tiled=True)]
    reduce_scatter x2, waiting for transfers between devices: 397 us -> 404 us  [body(): lax.psum_scatter(routed, 'region', scatter_dimension=1, tiled=True)]
where the time goes in v1:
time: 739 us
  waiting for transfers between devices  467 us (63%)
  blocking collectives  178 us (24%)
  matrix products  53 us (7%)
  between operations  16.2 us (2%)
  local copies, waits for them, and re-layouts  11.9 us (2%)
  other arithmetic  11.7 us (2%)
    reduce_scatter x2, waiting for transfers between devices, body(): lax.psum_scatter(routed, 'region', scatter_dimension=1, tiled=True)  404 us
    psum x1, blocking collectives, body(): cost_all, demand_all = lax.psum((cost_sq, demand_sq), ('region', 'comm'))  79.2 us
    psum x1, blocking collectives, body(): capacity_all = lax.psum(capacity_sq, 'region')  73.2 us
    all_gather x2, waiting for transfers between devices, body(): lax.all_gather(node_dual[:, :edge_cols], 'region', axis=1, tiled=True)  62.8 us
    dot_general x2, matrix products, body(): jnp.einsum('kba,bna->kbn', repeated_flow, incidence, precision=highest)  30.9 us
    all_gather x2, blocking collectives, body(): pieces = lax.all_gather(arc_load, 'comm', axis=0, tiled=False)  25.9 us
    dot_general x2, matrix products, body(): jnp.einsum('kbn,bna->kba', chosen_duals, incidence, precision=highest)  19.2 us
  transfers between devices with their start and end apart: 4, of which 3 were waited for; matrix products, arithmetic and copies ran while one was open for 1% of the time, Pallas kernels for 0%

profile of v1, /device:TPU:8, one launch (start us, length us, event | category | flops | bytes accessed | tf_op | source)
XLA Modules:
  0.0 738.6 jit_solution(11486823875616351913)
XLA Ops:
  7.2 1.5 slice.30
  8.8 1.6 multiply_reduce_fusion.1
  10.4 1.8 multiply_reduce_fusion
  12.2 1.4 multiply_reduce_fusion.2
  13.6 79.2 %all-reduce = (f32[]{:T(128)}, f32[]{:T(128)}) all-reduce(f32[]{:T(128)} %multiply_reduce_fusion, f32[]{:T(128)} %multiply_reduce_fusion.1), channel_id=1, replica_groups=mesh['region'=32,'comm'=8] {'region','comm'}, use_global_device_ids=true, to_apply=%region_1.0 | all-reduce | flops 2 | bytes 16 | tf_op jit(solution)/shard_map/psum | solution.py:38
  92.9 73.2 %psum.23 = f32[]{:T(128)} all-reduce(f32[]{:T(128)} %multiply_reduce_fusion.2), channel_id=1, replica_groups=mesh['region'=32,'comm'=8] {'region'}, use_global_device_ids=true, to_apply=%region_5.0 | all-reduce | flops 1 | bytes 8 | tf_op jit(solution)/shard_map/psum | solution.py:39
  168.2 0.7 compare_select_fusion.1
  168.8 0.7 compare_select_fusion
  169.5 0.7 compare_and_fusion
  170.1 0.7 compare_and_fusion.1
  170.8 1.0 copy_bitcast_fusion.5
  171.8 1.3 copy_bitcast_fusion.1
  173.1 0.6 gather_fusion
  173.7 0.1 select_bitcast_fusion.1
  173.8 0.8 gather_fusion.1
  174.6 9.6 %bitcast_reduce_fusion.1 = f32[16,64,128]{2,0,1:T(8,128)S(1)} fusion(f32[128,128,128]{2,1,0:T(8,128)} %param.19, f32[128,16,128]{2,1,0:T(8,128)S(1)} %gather_fusion.1, pred[128]{0:T(512)(128)(4,1)S(1)} %compare_and_fusion), kind=kOutput, calls=%fused_computation.13 | convolution fusion | flops 403046400 | bytes 9961600 | tf_op jit(solution)/shard_map/kbn,bna->kba/dot_general | solution.py:58
  184.2 0.2 fusion.28
  184.5 0.1 copy_bitcast_fusion.3
  184.5 0.1 broadcast_in_dim.30
  184.7 15.4 %convolution_bitcast_fusion.1 = f32[16,128,128]{2,0,1:T(8,128)S(1)} fusion(f32[16,128,128]{2,0,1:T(8,128)S(1)} %bitcast.122, f32[128,128,128]{2,1,0:T(8,128)} %param.19), kind=kOutput, calls=%fused_computation.5 | convolution fusion | flops 402653184 | bytes 10485760 | tf_op jit(solution)/shard_map/kba,bna->kbn/dot_general | solution.py:73
  200.1 0.8 convolution_bitcast_fusion.5
  200.9 0.7 convolution_bitcast_fusion.3
  201.6 1.6 copy.51
  203.3 206.3 %reduce-scatter.3.cloned.1.call-done = f32[16,4,128]{2,0,1:T(8,128)} async-done(((f32[16,128,128]{2,0,1:T(8,128)}), f32[16,4,128]{2,0,1:T(8,128)}) %reduce-scatter.3.cloned.1.call-update) | async-done | bytes 32784 | tf_op jit(solution)/shard_map/reduce_scatter | solution.py:79
  409.6 0.8 slice_add_fusion.1
  410.4 0.2 fusion.27
  410.6 0.6 slice.49
  411.3 13.1 %all-gather = f32[65536]{0:T(1024)S(1)} all-gather(f32[8192]{0:T(1024)S(1)} %get-tuple-element.9), channel_id=2, replica_groups=mesh['region'=32,'comm'=8] {'comm'}, dimensions={0}, use_global_device_ids=true | all-gather | bytes 294912 | tf_op jit(solution)/shard_map/all_gather | solution.py:67
  424.4 0.1 reduce_sum.87
  424.6 62.7 %all-gather.7.cloned.1.call-done = f32[16,16384]{1,0:T(8,128)} async-done(((f32[16,512]{1,0:T(8,128)}), f32[16,16384]{1,0:T(8,128)}) %all-gather.7.cloned.1.call-update) | async-done | bytes 1048592 | tf_op jit(solution)/shard_map/all_gather | solution.py:52
  487.3 1.3 copy_bitcast_fusion
  488.6 0.6 gather_fusion.2
  489.2 0.1 select_bitcast_fusion
  489.3 0.8 gather_fusion.3
  490.1 9.6 %bitcast_reduce_fusion = f32[16,64,128]{2,0,1:T(8,128)S(1)} fusion(f32[128,128,128]{2,1,0:T(8,128)} %param.19, f32[128,16,128]{2,1,0:T(8,128)S(1)} %gather_fusion.3, pred[128]{0:T(512)(128)(4,1)S(1)} %compare_and_fusion), kind=kOutput, calls=%fused_computation.12 | convolution fusion | flops 403046400 | bytes 9961600 | tf_op jit(solution)/shard_map/kbn,bna->kba/dot_general | solution.py:58
  499.7 0.2 fusion.30
  499.9 0.1 broadcast_in_dim.31
  500.0 15.4 %convolution_bitcast_fusion = f32[16,128,128]{2,0,1:T(8,128)S(1)} fusion(f32[16,128,128]{2,0,1:T(8,128)S(1)} %bitcast.123, f32[128,128,128]{2,1,0:T(8,128)} %param.19), kind=kOutput, calls=%fused_computation.4 | convolution fusion | flops 402653184 | bytes 10485760 | tf_op jit(solution)/shard_map/kba,bna->kbn/dot_general | solution.py:73
  515.4 0.8 convolution_bitcast_fusion.4
  516.2 0.7 convolution_bitcast_fusion.2
  516.9 1.6 copy.58
  518.5 0.1 fusion.31
  518.7 12.9 %all-gather.1 = f32[65536]{0:T(1024)S(1)} all-gather(f32[8192]{0:T(1024)S(1)} %fusion.31), channel_id=3, replica_groups=mesh['region'=32,'comm'=8] {'comm'}, dimensions={0}, use_global_device_ids=true | all-gather | bytes 294912 | tf_op jit(solution)/shard_map/all_gather | solution.py:67
  531.6 0.1 reduce_sum.89
  531.7 0.6 add_maximum_fusion
  532.3 198.0 %reduce-scatter.5.cloned.1.call-done = f32[16,4,128]{2,0,1:T(8,128)} async-done(((f32[16,128,128]{2,0,1:T(8,128)}), f32[16,4,128]{2,0,1:T(8,128)}) %reduce-scatter.5.cloned.1.call-update) | async-done | bytes 32784 | tf_op jit(solution)/shard_map/reduce_scatter | solution.py:79
  730.3 0.8 slice_add_fusion
  731.1 0.9 fusion.25
  (40 shorter events, 0.6 us)
Async XLA Ops:
  7.2 177.0 %copy-start = (f32[16,8192]{1,0:T(8,128)S(1)}, f32[16,8192]{1,0:T(8,128)}, u32[]{:S(2)}) copy-start(f32[16,8192]{1,0:T(8,128)} %param.13) | copy-start | bytes 1572868
  7.2 177.0 %copy-start.6 = (f32[8192]{0:T(1024)S(1)}, f32[8192]{0:T(1024)}, u32[]{:S(2)}) copy-start(f32[8192]{0:T(1024)} %param.16) | copy-start | bytes 98308
  7.2 177.0 %copy-start.2 = (f32[16,8192]{1,0:T(8,128)S(1)}, f32[16,8192]{1,0:T(8,128)}, u32[]{:S(2)}) copy-start(f32[16,8192]{1,0:T(8,128)} %param.14) | copy-start | bytes 1572868
  7.2 164.6 %all-gather.5.cloned.1.call-start = ((), (), s32[]{:S(2)}) async-start(), calls=%async_computation.2 | async-start | bytes 1081344 | tf_op jit(solution)/shard_map/all_gather | solution.py:52
  8.7 400.9 %reduce-scatter.3.cloned.1.call-start = ((), (), s32[]{:S(2)}) async-start(), calls=%async_computation.3 | async-start | bytes 1081344 | tf_op jit(solution)/shard_map/reduce_scatter | solution.py:79
  184.2 15.9 %copy-start.7 = (s32[128]{0:T(128)S(1)}, s32[128]{0:T(128)}, u32[]{:S(2)}) copy-start(s32[128]{0:T(128)} %param.20) | copy-start | bytes 1540
  184.2 16.6 %copy-start.8 = (s32[8]{0:T(128)S(1)}, s32[8]{0:T(128)}, u32[]{:S(2)}) copy-start(s32[8]{0:T(128)} %param.21) | copy-start | bytes 100
  184.6 225.8 %copy-start.1 = (f32[16,4096]{1,0:T(8,128)S(1)}, f32[16,4096]{1,0:T(8,128)}, u32[]{:S(2)}) copy-start(f32[16,4096]{1,0:T(8,128)} %param.17) | copy-start | bytes 786436
  184.6 225.8 %copy-start.4 = (f32[16,4096]{1,0:T(8,128)S(1)}, f32[16,4096]{1,0:T(8,128)}, u32[]{:S(2)}) copy-start(f32[16,4096]{1,0:T(8,128)} %param.18) | copy-start | bytes 786436
  184.6 239.9 %copy-start.5 = (f32[8192]{0:T(1024)S(1)}, f32[8192]{0:T(1024)}, u32[]{:S(2)}) copy-start(f32[8192]{0:T(1024)} %param.15) | copy-start | bytes 98308
  203.2 284.1 %all-gather.7.cloned.1.call-start = ((), (), s32[]{:S(2)}) async-start(), calls=%async_computation.4 | async-start | bytes 1081344 | tf_op jit(solution)/shard_map/all_gather | solution.py:52
  411.3 319.1 %reduce-scatter.5.cloned.1.call-start = ((), (), s32[]{:S(2)}) async-start(), calls=%async_computation.5 | async-start | bytes 1081344 | tf_op jit(solution)/shard_map/reduce_scatter | solution.py:79
  499.8 18.7 %copy-start.3 = (f32[16,8192]{1,0:T(8,128)}, f32[16,8192]{1,0:T(8,128)S(1)}, u32[]{:S(2)}) copy-start(f32[16,8192]{1,0:T(8,128)S(1)} %get-tuple-element.8) | copy-start | bytes 1572868
Sparse Core Ops, SparseCore 0:
  11.2 78.9 all-gather.4
  203.3 206.2 reduce-scatter.2
  412.8 74.4 all-gather.6
  518.6 211.6 reduce-scatter.4
